TPU v7x, 32 devices: a whole 2x2x4 slice. The times are simulated.
32 devices in a mesh: ctx: 8 (over z, core), tp: 4 (over y, x).
Axes of the slice: x: 2, y: 2, z: 4, core: 2. Of those that a mesh axis runs over, the one named last changes fastest.
Arguments:
- tokens: bfloat16 [4096, 4096], P(('ctx', 'tp')), may hold values from -6 to 6
- in_weight: bfloat16 [3, 4096, 2048], P(None, None, 'tp'), may hold values from -0.09375 to 0.09375
- short_taps: float32 [3, 3, 2048], P(None, None, 'tp'), may hold values from -3 to 3
- decay_rate: float32 [16, 2048], P(None, 'tp'), may hold values from 4.8828125e-05 to 0.0333333333
- residue: float32 [16, 2048], P(None, 'tp'), may hold values from -0.26 to 0.26
- skip_gain: float32 [2048], P('tp'), may hold values from -4 to 4
- grad_out: bfloat16 [4096, 2048], P('ctx', 'tp'), may hold values from -6 to 6
Outputs:
- mixed_out: bfloat16 [4096, 2048], P('ctx', 'tp')
- input_grad: bfloat16 [4096, 4096], P(('ctx', 'tp'))
All inputs are finite; a program needn't handle non-finite values.
Results may differ from a plain program's by a relative error of at most 0.0065.
Values may be sent and summed in bfloat16 or wider, within the bound.
A program may use at most 192 MiB of HBM per device.

v0:
```python
import jax
import jax.numpy as jnp
from jax import lax
from jax.sharding import PartitionSpec as P

exact_mode = lax.Precision.HIGHEST


def from_behind(value, axis, steps):
    count = lax.axis_size(axis)
    leading, last = (max(0, -steps), min(count, count - steps))
    return lax.ppermute(value, axis, [(source, source + steps) for source in range(leading, last)])


def modal_block(signal, log_pole, residue):
    length, channels = signal.shape
    sub_len = min(64, length)
    sub_count = length // sub_len
    offsets = jnp.arange(sub_len, dtype=jnp.float32)
    sections = signal.reshape(sub_count, sub_len, channels)
    powers = jnp.exp(log_pole[:, None, :] * offsets[None, :, None])
    filter_taps = jnp.sum(residue[:, None, :] * powers, axis=0)
    lag_index = jnp.arange(sub_len)[:, None] - jnp.arange(sub_len)[None, :]
    toeplitz = jnp.where((lag_index >= 0)[:, :, None], filter_taps[jnp.maximum(lag_index, 0)], 0.0)
    within = jnp.einsum("abc,kbc->kac", toeplitz, sections, precision=exact_mode)
    to_end = jnp.exp(log_pole[:, None, :] * (sub_len - 1.0 - offsets)[None, :, None])
    end_states = jnp.einsum("nbc,kbc->nkc", to_end, sections, precision=exact_mode)
    lag_blocks = jnp.arange(sub_count + 1)[:, None] - 1 - jnp.arange(sub_count)[None, :]
    valid_lag = lag_blocks >= 0
    lag_float = (jnp.maximum(lag_blocks, 0) * sub_len).astype(jnp.float32)
    decay_table = jnp.exp(log_pole[None, None] * lag_float[:, :, None, None])
    decay_table = jnp.where(valid_lag[:, :, None, None], decay_table, 0.0)
    carried = jnp.einsum("kmnc,nmc->nkc", decay_table, end_states, precision=exact_mode)
    stepped = residue[:, None, :] * jnp.exp(log_pole[:, None, :] * (offsets[None, :, None] + 1.0))
    output = within + jnp.einsum(
        "nac,nkc->kac", stepped, carried[:, :sub_count], precision=exact_mode
    )
    return (output.reshape(length, channels), carried[:, sub_count])


def carry_term(incoming, log_pole, residue, length):
    channels = incoming.shape[1]
    sub_len = min(64, length)
    sub_count = length // sub_len
    offsets = jnp.arange(sub_len, dtype=jnp.float32)
    stepped = residue[:, None, :] * jnp.exp(log_pole[:, None, :] * (offsets[None, :, None] + 1.0))
    block_starts = (jnp.arange(sub_count) * sub_len).astype(jnp.float32)
    start_states = incoming[:, None, :] * jnp.exp(
        log_pole[:, None, :] * block_starts[None, :, None]
    )
    output = jnp.einsum("nac,nkc->kac", stepped, start_states, precision=exact_mode)
    return output.reshape(length, channels)


def shards(tokens, in_weight, short_taps, decay_rate, residue, skip_gain, grad_out):
    width = in_weight.shape[2]
    weight_cat = jnp.concatenate([in_weight[0], in_weight[1], in_weight[2]], axis=1)
    streams = jnp.dot(
        lax.all_gather(tokens, "tp", axis=0, tiled=True),
        weight_cat,
        preferred_element_type=jnp.float32,
    ).astype(jnp.bfloat16)
    length = streams.shape[0]
    tap_reach = short_taps.shape[1] - 1
    taps_cat = jnp.concatenate([short_taps[0], short_taps[1], short_taps[2]], axis=1)
    before = from_behind(streams[length - tap_reach :], "ctx", 1)
    extended = jnp.concatenate([before, streams], axis=0).astype(jnp.float32)
    short_mixed = taps_cat[0][None] * extended[tap_reach:]
    for offset in range(1, tap_reach + 1):
        short_mixed = (
            short_mixed
            + taps_cat[offset][None] * extended[tap_reach - offset : tap_reach - offset + length]
        )
    query_side = short_mixed[:, :width]
    key_side = short_mixed[:, width : 2 * width]
    value_side = short_mixed[:, 2 * width :]
    product_in = key_side * value_side
    log_pole = -decay_rate
    forward_local, forward_sum = modal_block(product_in, log_pole, residue)
    upstream = grad_out.astype(jnp.float32)
    conv_grad = upstream * query_side
    backward_local, backward_sum = modal_block(conv_grad[::-1], log_pole, residue)
    position = lax.axis_index("ctx")
    summaries = (
        lax.all_gather(forward_sum[None], "ctx", axis=0, tiled=True),
        lax.all_gather(backward_sum[None], "ctx", axis=0, tiled=True),
    )
    block_index = jnp.arange(summaries[0].shape[0])
    earlier_gap = position - 1 - block_index
    later_gap = block_index - position - 1
    scale_fwd = (jnp.maximum(earlier_gap, 0) * length).astype(jnp.float32)
    scale_bwd = (jnp.maximum(later_gap, 0) * length).astype(jnp.float32)
    weight_fwd = jnp.where(
        (earlier_gap >= 0)[:, None, None], jnp.exp(log_pole[None] * scale_fwd[:, None, None]), 0.0
    )
    weight_bwd = jnp.where(
        (later_gap >= 0)[:, None, None], jnp.exp(log_pole[None] * scale_bwd[:, None, None]), 0.0
    )
    incoming_fwd = jnp.sum(weight_fwd * summaries[0], axis=0)
    incoming_bwd = jnp.sum(weight_bwd * summaries[1], axis=0)
    conv_out = forward_local + carry_term(incoming_fwd, log_pole, residue, length)
    back_conv = (backward_local + carry_term(incoming_bwd, log_pole, residue, length))[::-1]
    filtered = conv_out + skip_gain[None] * product_in
    result = (query_side * filtered).astype(jnp.bfloat16)
    grad_query = upstream * filtered
    grad_product = back_conv + skip_gain[None] * conv_grad
    stream_grads = jnp.concatenate(
        [grad_query, grad_product * value_side, grad_product * key_side], axis=1
    )
    after_rows = from_behind(stream_grads[:tap_reach], "ctx", -1)
    padded = jnp.concatenate([stream_grads, after_rows], axis=0)
    grad_streams = taps_cat[0][None] * padded[:length]
    for offset in range(1, tap_reach + 1):
        grad_streams = grad_streams + taps_cat[offset][None] * padded[offset : offset + length]
    grad_streams = grad_streams.astype(jnp.bfloat16)
    input_grad = lax.psum_scatter(
        jnp.einsum("rk,dk->rd", grad_streams, weight_cat, preferred_element_type=jnp.float32),
        "tp",
        scatter_dimension=0,
        tiled=True,
    )
    return (result, input_grad.astype(jnp.bfloat16))


def solution(mesh):
    in_specs = (
        P(("ctx", "tp"), None),
        P(None, None, "tp"),
        P(None, None, "tp"),
        P(None, "tp"),
        P(None, "tp"),
        P("tp"),
        P("ctx", "tp"),
    )
    out_specs = (P("ctx", "tp"), P(("ctx", "tp"), None))
    return jax.shard_map(shards, mesh=mesh, in_specs=in_specs, out_specs=out_specs, check_vma=False)
```

profile of v0, /device:TPU:0, one launch (start us, length us, event | category | flops | bytes accessed | tf_op | source)
XLA Modules:
  0.0 426.4 jit_solution(13734944484443830677)
XLA Ops:
  10.8 6.0 %multiply_reduce_fusion = f32[64,512]{0,1:T(8,128)S(1)} fusion(f32[16,512]{0,1:T(8,128)S(1)} %copy.29, f32[16,512]{0,1:T(8,128)S(1)} %copy.28), kind=kLoop, calls=%fused_computation.20 | loop fusion | flops 1540096 | bytes 196608 | tf_op jit(solution)/shard_map/reduce_sum | solution.py:22
  16.8 10.3 %slice_bitcast_fusion.2 = (bf16[4096,512]{1,0:T(8,128)(2,1)}, bf16[4096,512]{1,0:T(8,128)(2,1)}, bf16[4096,512]{1,0:T(8,128)(2,1)}) fusion(bf16[3,4096,512]{2,1,0:T(8,128)(2,1)} %param.8), kind=kLoop, calls=%fused_computation.23 | loop fusion | bytes 25165824 | tf_op jit(solution)/shard_map/squeeze | solution.py:57
  27.1 38.0 %all-gather.4.cloned.1.call-done = bf16[512,4096]{1,0:T(8,128)(2,1)} async-done(((bf16[128,4096]{1,0:T(8,128)(2,1)}), bf16[512,4096]{1,0:T(8,128)(2,1)}) %all-gather.4.cloned.1.call-update) | async-done | bytes 4194320 | tf_op jit(solution)/shard_map/all_gather | solution.py:59
  65.1 12.5 %fusion.22 = bf16[512,1536]{1,0:T(8,128)(2,1)S(1)} fusion(bf16[512,4096]{1,0:T(8,128)(2,1)} %all-gather.4.cloned.1.call-done, bf16[4096,512]{1,0:T(8,128)(2,1)} %get-tuple-element.10, bf16[4096,512]{1,0:T(8,128)(2,1)} %get-tuple-element.11, bf16[4096,512]{1,0:T(8,128)(2,1)} %get-tuple-element.9), kind=kOutput, calls=%fused_computation.37 | convolution fusion | flops 6480986112 | bytes 18350080 | tf_op jit(solution)/shard_map/dot_general | solution.py:58
  79.7 16.8 %gather_fusion = f32[4096,512]{1,0:T(8,128)} fusion(f32[64,512]{1,0:T(8,128)S(1)} %copy.30, s32[4096]{0:T(1024)S(1)} %broadcast_clamp_fusion), kind=kCustom, calls=%fused_computation | custom fusion | bytes 16793600 | tf_op jit(solution)/shard_map/gather | solution.py:24
  96.5 16.3 %copy.31 = f32[64,64,512]{1,0,2:T(8,128)} copy(f32[64,64,512]{2,1,0:T(8,128)} %bitcast.51) | data formatting | bytes 16777216 | tf_op jit(solution)/shard_map/gather | solution.py:24
  116.1 8.9 %rev.6 = f32[512,512]{1,0:T(8,128)} reverse(f32[512,512]{1,0:T(8,128)} %get-tuple-element.15), dimensions={0} | reverse | bytes 2097152 | tf_op jit(solution)/shard_map/rev | solution.py:82
  131.4 9.5 %fusion.43 = f32[16,512,8]{0,2,1:T(8,128)} fusion(f32[8,64,512]{1,0,2:T(8,128)} %copy.32, f32[64]{0:T(128)S(1)} %iota_subtract_fusion.2, f32[16,512]{0,1:T(8,128)S(1)} %copy.29), kind=kOutput, calls=%fused_computation.64 | convolution fusion | flops 50855936 | bytes 1343744 | tf_op jit(solution)/shard_map/nbc,kbc->nkc/dot_general | solution.py:27
  140.9 30.5 %fusion.2 = f32[512,8,64]{2,1,0:T(8,128)} fusion(f32[8,64,512]{1,0,2:T(8,128)S(1)} %copy-done.1, f32[64,64,512]{1,0,2:T(8,128)} %copy.31, pred[64,64]{1,0:T(8,128)(4,1)S(1)} %subtract_compare_fusion), kind=kOutput, calls=%fused_computation.3 | convolution fusion | flops 203423744 | bytes 10489856 | tf_op jit(solution)/shard_map/abc,kbc->kac/dot_general | solution.py:25
  171.3 30.2 %fusion = f32[512,8,64]{2,1,0:T(8,128)} fusion(f32[8,64,512]{1,0,2:T(8,128)S(1)} %copy-done, f32[64,64,512]{1,0,2:T(8,128)} %copy.31, pred[64,64]{1,0:T(8,128)(4,1)S(1)} %subtract_compare_fusion), kind=kOutput, calls=%fused_computation.1 | convolution fusion | flops 203423744 | bytes 10489856 | tf_op jit(solution)/shard_map/abc,kbc->kac/dot_general | solution.py:25
  201.5 8.3 %fusion.44 = f32[16,512,8]{0,2,1:T(8,128)} fusion(f32[8,64,512]{1,0,2:T(8,128)S(1)} %copy-done, f32[64]{0:T(128)S(1)} %iota_subtract_fusion.2, f32[16,512]{0,1:T(8,128)S(1)} %copy.29), kind=kOutput, calls=%fused_computation.65 | convolution fusion | flops 50855936 | bytes 1343744 | tf_op jit(solution)/shard_map/nbc,kbc->nkc/dot_general | solution.py:27
  218.4 4.5 %copy.58 = f32[16,512,9]{0,2,1:T(8,128)} copy(f32[16,512,9]{1,0,2:T(8,128)} %get-tuple-element.2) | data formatting | bytes 589824 | tf_op jit(solution)/shard_map/kmnc,nmc->nkc/dot_general | solution.py:33
  226.3 14.7 %all-gather.1 = f32[128,1,512]{2,1,0:T(1,128)S(1)} all-gather(f32[16,1,512]{2,1,0:T(1,128)S(1)} %copy.40), channel_id=3, replica_groups=mesh['ctx'=8,'tp'=4] {'ctx'}, dimensions={0}, use_global_device_ids=true | all-gather | bytes 294912 | tf_op jit(solution)/shard_map/all_gather | solution.py:86
  241.7 4.5 %copy.50 = f32[16,512,9]{0,2,1:T(8,128)} copy(f32[16,512,9]{1,0,2:T(8,128)} %get-tuple-element.3) | data formatting | bytes 589824 | tf_op jit(solution)/shard_map/kmnc,nmc->nkc/dot_general | solution.py:33
  249.7 14.2 %all-gather = f32[128,1,512]{2,1,0:T(1,128)S(1)} all-gather(f32[16,1,512]{2,1,0:T(1,128)S(1)} %copy.34), channel_id=2, replica_groups=mesh['ctx'=8,'tp'=4] {'ctx'}, dimensions={0}, use_global_device_ids=true | all-gather | bytes 294912 | tf_op jit(solution)/shard_map/all_gather | solution.py:85
  266.7 6.8 %fusion.12 = f32[512,8,64]{2,1,0:T(8,128)S(1)} fusion(f32[64]{0:T(128)S(1)} %iota_add_fusion, f32[16,512]{0,1:T(8,128)S(1)} %copy.29, f32[16,512]{0,1:T(8,128)} %copy-done.9, f32[8]{0:T(128)S(1)} %multiply_convert_fusion.3, f32[16,512]{0,1:T(8,128)} %copy.35), kind=kOutput, calls=%fused_computation.15 | convolution fusion | flops 51511296 | bytes 1147168 | tf_op jit(solution)/shard_map/nac,nkc->kac/dot_general | solution.py:51
  273.5 6.5 %add_bitcast_fusion.1 = f32[8,64,512]{1,0,2:T(8,128)} fusion(f32[512,8,64]{2,1,0:T(8,128)S(1)} %fusion.12, f32[512,8,64]{2,1,0:T(8,128)S(1)} %copy-done.8, f32[64]{0:T(128)S(1)} %iota_add_fusion, f32[16,512]{0,1:T(8,128)S(1)} %copy.29, f32[16,512]{0,1:T(8,128)S(1)} %copy-done.10, f32[16,9,512]{0,1,2:T(8,128)S(1)} %bitcast.55), kind=kOutput, calls=%fused_computation.45 | convolution fusion | flops 51904512 | bytes 7864832 | tf_op jit(solution)/shard_map/nac,nkc->kac/dot_general | solution.py:35
  283.2 6.5 %fusion.10 = f32[512,8,64]{2,1,0:T(8,128)S(1)} fusion(f32[64]{0:T(128)S(1)} %iota_add_fusion, f32[16,512]{0,1:T(8,128)S(1)} %copy.29, f32[16,512]{0,1:T(8,128)} %copy-done.9, f32[16,512]{0,1:T(8,128)} %copy.41, f32[8]{0:T(128)S(1)} %multiply_convert_fusion.3), kind=kOutput, calls=%fused_computation.13 | convolution fusion | flops 51511296 | bytes 1147168 | tf_op jit(solution)/shard_map/nac,nkc->kac/dot_general | solution.py:51
  289.7 6.5 %add_bitcast_fusion = f32[8,64,512]{1,0,2:T(8,128)} fusion(f32[512,8,64]{2,1,0:T(8,128)S(1)} %fusion.10, f32[512,8,64]{2,1,0:T(8,128)S(1)} %copy-done.7, f32[64]{0:T(128)S(1)} %iota_add_fusion, f32[16,512]{0,1:T(8,128)S(1)} %copy.29, f32[16,512]{0,1:T(8,128)S(1)} %copy-done.11, f32[16,9,512]{0,1,2:T(8,128)S(1)} %bitcast.53), kind=kOutput, calls=%fused_computation.43 | convolution fusion | flops 51904512 | bytes 7864832 | tf_op jit(solution)/shard_map/nac,nkc->kac/dot_general | solution.py:35
  296.2 3.2 copy.42
  299.4 8.9 %rev.7 = f32[512,512]{1,0:T(8,128)} reverse(f32[512,512]{1,0:T(8,128)} %bitcast.57), dimensions={0} | reverse | bytes 2097152 | tf_op jit(solution)/shard_map/rev | solution.py:102
  308.4 4.1 slice_multiply_fusion.5
  315.9 13.4 %fusion.8 = f32[512,4096]{1,0:T(8,128)} fusion(bf16[4096,512]{1,0:T(8,128)(2,1)} %get-tuple-element.10, bf16[4096,512]{1,0:T(8,128)(2,1)} %get-tuple-element.11, bf16[4096,512]{1,0:T(8,128)(2,1)} %get-tuple-element.9, f32[514,1536]{1,0:T(8,128)S(1)} %pad_maximum_fusion.3, f32[1536]{0:T(1024)S(1)} %get-tuple-element.8, f32[1536]{0:T(1024)S(1)} %get-tuple-element.7, ...), kind=kOutput, calls=%fused_computation.10 | convolution fusion | flops 6486491136 | bytes 30433280 | tf_op jit(solution)/shard_map/rk,dk->rd/dot_general | solution.py:117
  329.4 86.9 %reduce-scatter.2.cloned.1.call-done = f32[128,4096]{1,0:T(8,128)} async-done(((f32[512,4096]{1,0:T(8,128)}), f32[128,4096]{1,0:T(8,128)}) %reduce-scatter.2.cloned.1.call-update) | async-done | bytes 2097168 | tf_op jit(solution)/shard_map/reduce_scatter | solution.py:116
  (77 shorter events, 43.7 us)
Async XLA Ops:
  7.2 58.0 %all-gather.4.cloned.1.call-start = ((), (), s32[]{:S(2)}) async-start(), calls=%async_computation.1 | async-start | bytes 5242880 | tf_op jit(solution)/shard_map/all_gather | solution.py:59
  7.9 408.4 %reduce-scatter.2.cloned.1.call-start = ((), (), s32[]{:S(2)}) async-start(), calls=%async_computation.2 | async-start | bytes 10485760 | tf_op jit(solution)/shard_map/reduce_scatter | solution.py:116
  9.8 17.3 %copy-start.9 = (f32[16,512]{0,1:T(8,128)}, f32[16,512]{0,1:T(8,128)S(1)}, u32[]{:S(2)}) copy-start(f32[16,512]{0,1:T(8,128)S(1)} %copy.28) | copy-start | bytes 98308
  77.7 35.2 %collective-permute-start = (bf16[2,1536]{1,0:T(2,128)(2,1)S(1)}, bf16[2,1536]{1,0:T(2,128)(2,1)S(1)}, u32[]{:S(2)}, u32[]{:S(2)}) collective-permute-start(bf16[2,1536]{1,0:T(2,128)(2,1)S(1)} %slice.97), channel_id=1, source_target_pairs={{0,4},{4,8},{8,12},{12,16},{16,20},{20,24},{24,28},{1,5},{5,9},{9,... | collective-permute-start | bytes 18440 | tf_op jit(solution)/shard_map/ppermute | solution.py:12
  113.3 1.0 copy-start.12
  131.4 9.5 %copy-start.1 = (f32[8,64,512]{1,0,2:T(8,128)S(1)}, f32[8,64,512]{1,0,2:T(8,128)}, u32[]{:S(2)}) copy-start(f32[8,64,512]{1,0,2:T(8,128)} %copy.32) | copy-start | bytes 3145732
  140.8 30.5 %copy-start = (f32[8,64,512]{1,0,2:T(8,128)S(1)}, f32[8,64,512]{1,0,2:T(8,128)}, u32[]{:S(2)}) copy-start(f32[8,64,512]{1,0,2:T(8,128)} %copy.38) | copy-start | bytes 3145732
  266.7 6.8 %copy-start.3 = (f32[16,512,9]{0,2,1:T(8,128)S(1)}, f32[16,512,9]{0,2,1:T(8,128)}, u32[]{:S(2)}) copy-start(f32[16,512,9]{0,2,1:T(8,128)} %copy.50) | copy-start | bytes 884740
  266.7 6.8 %copy-start.8 = (f32[512,8,64]{2,1,0:T(8,128)S(1)}, f32[512,8,64]{2,1,0:T(8,128)}, u32[]{:S(2)}) copy-start(f32[512,8,64]{2,1,0:T(8,128)} %fusion.2) | copy-start | bytes 3145732
  266.7 6.8 %copy-start.10 = (f32[16,512]{0,1:T(8,128)S(1)}, f32[16,512]{0,1:T(8,128)}, u32[]{:S(2)}) copy-start(f32[16,512]{0,1:T(8,128)} %copy-done.9) | copy-start | bytes 98308
  283.2 6.5 %copy-start.2 = (f32[16,512,9]{0,2,1:T(8,128)S(1)}, f32[16,512,9]{0,2,1:T(8,128)}, u32[]{:S(2)}) copy-start(f32[16,512,9]{0,2,1:T(8,128)} %copy.58) | copy-start | bytes 884740
  283.2 6.5 %copy-start.7 = (f32[512,8,64]{2,1,0:T(8,128)S(1)}, f32[512,8,64]{2,1,0:T(8,128)}, u32[]{:S(2)}) copy-start(f32[512,8,64]{2,1,0:T(8,128)} %fusion) | copy-start | bytes 3145732
  283.2 6.5 %copy-start.11 = (f32[16,512]{0,1:T(8,128)S(1)}, f32[16,512]{0,1:T(8,128)}, u32[]{:S(2)}) copy-start(f32[16,512]{0,1:T(8,128)} %copy-done.9) | copy-start | bytes 98308
  296.2 12.1 %copy-start.13 = (f32[512]{0:T(512)S(1)}, f32[512]{0:T(512)}, u32[]{:S(2)}) copy-start(f32[512]{0:T(512)} %param.12) | copy-start | bytes 6148
  312.4 3.3 copy-start.4
  312.4 3.3 copy-start.5
  312.4 3.3 copy-start.6
  312.6 3.1 collective-permute-start.1
Sparse Core Ops, SparseCore 0:
  9.8 55.2 all-gather.3
  329.5 86.7 reduce-scatter.1
where the time goes:
time: 433 us; the launch traced here: 426 us
  matrix products  131 us (30%)
  waiting for transfers between devices  127 us (29%)
  local copies, waits for them, and re-layouts  100 us (23%)
  blocking collectives  28.9 us (7%)
  other arithmetic  21.2 us (5%)
  between operations  14.8 us (3%)
    reduce_scatter x1, waiting for transfers between devices, shards(): lax.psum_scatter(jnp.einsum('rk,dk->rd', grad_streams, weight_cat, prefer...  86.9 us
    dot_general x2, matrix products, modal_block(): jnp.einsum('abc,kbc->kac', toeplitz, sections, precision=exact_mode)  60.7 us
    all_gather x1, waiting for transfers between devices, shards(): lax.all_gather(tokens, 'tp', axis=0, tiled=True)  38 us
    gather x2, local copies, waits for them, and re-layouts, modal_block(): filter_taps[jnp.maximum(lag_index, 0)]  33.1 us
    dot_general x2, matrix products, modal_block(): jnp.einsum('nbc,kbc->nkc', to_end, sections, precision=exact_mode)  17.8 us
    all_gather x1, blocking collectives, shards(): lax.all_gather(backward_sum[None], 'ctx', axis=0, tiled=True)  14.7 us
    all_gather x1, blocking collectives, shards(): lax.all_gather(forward_sum[None], 'ctx', axis=0, tiled=True)  14.2 us
    dot_general x1, matrix products, shards(): jnp.einsum('rk,dk->rd', grad_streams, weight_cat, preferred_element_type=...  13.4 us
  transfers between devices with their start and end apart: 4, of which 3 were waited for; matrix products, arithmetic and copies ran while one was open for 12% of the time, Pallas kernels for 0%

commit v1 on v0

--- a/solution.py
+++ b/solution.py
@@ -1,6 +1,10 @@
+import functools
+
 import jax
 import jax.numpy as jnp
 from jax import lax
+from jax.experimental import pallas as pl
+from jax.experimental.pallas import tpu as pltpu
 from jax.sharding import PartitionSpec as P
 
 exact_mode = lax.Precision.HIGHEST
@@ -122,6 +126,496 @@
     return (result, input_grad.astype(jnp.bfloat16))
 
 
+MESH = pl.DeviceIdType.MESH
+SUBLANES = 8
+LANES = 128
+ROWS = 32
+VMEM_LIMIT = 60 * 1024 * 1024
+
+
+def vmem_specs(count):
+    return [pl.BlockSpec(memory_space=pltpu.VMEM)] * count
+
+
+def square_partners():
+    me = lax.axis_index("tp")
+    y, x = me // 2, me % 2
+    return me, y * 2 + (1 - x), (1 - y) * 2 + x, (1 - y) * 2 + (1 - x)
+
+
+def greet(axis, partners):
+    barrier = pltpu.get_barrier_semaphore()
+    for partner in partners:
+        pl.semaphore_signal(barrier, inc=1, device_id={axis: partner}, device_id_type=MESH)
+    pl.semaphore_wait(barrier, len(partners))
+
+
+def project_kernel(tok_ref, w_hbm, out_ref, held, w_buf, w_sem, send_sem, recv_sem):
+    rows = tok_ref.shape[0]
+    half = rows // 2
+    width = w_hbm.shape[2]
+    tile = w_buf.shape[2]
+    per_stream = width // tile
+    me, xn, yn, dg = square_partners()
+    loads = []
+    for part in range(3 * per_stream):
+        stream, col = divmod(part, per_stream)
+        load = pltpu.make_async_copy(
+            w_hbm.at[stream, :, pl.ds(col * tile, tile)], w_buf.at[part], w_sem.at[part]
+        )
+        load.start()
+        loads.append(load)
+    greet("tp", (xn, yn))
+
+    def send(index, source, slot, start, partner):
+        return pltpu.make_async_remote_copy(
+            src_ref=source,
+            dst_ref=held.at[slot, pl.ds(start, half)],
+            send_sem=send_sem.at[index],
+            recv_sem=recv_sem.at[index],
+            device_id={"tp": partner},
+            device_id_type=MESH,
+        )
+
+    own_a, own_b = tok_ref.at[pl.ds(0, half)], tok_ref.at[pl.ds(half, half)]
+    copies = [
+        send(0, own_a, 0, 0, xn),
+        send(1, own_b, 1, half, yn),
+        send(2, own_b, 0, half, xn),
+        send(3, own_a, 1, 0, yn),
+        send(4, held.at[0, pl.ds(0, half)], 2, 0, yn),
+        send(5, held.at[1, pl.ds(half, half)], 2, half, xn),
+    ]
+    for index in range(4):
+        copies[index].start()
+
+    def multiply(block, owner):
+        start = pl.multiple_of(owner * rows, rows)
+
+        @pl.loop(0, 3 * per_stream)
+        def _(part):
+            out_ref[part, pl.ds(start, rows), :] = jnp.dot(
+                block[...], w_buf[part], preferred_element_type=jnp.float32
+            ).astype(out_ref.dtype)
+
+    for load in loads:
+        load.wait()
+    multiply(tok_ref, me)
+    copies[0].wait_recv()
+    copies[4].start()
+    copies[1].wait_recv()
+    copies[5].start()
+    copies[2].wait_recv()
+    multiply(held.at[0], xn)
+    copies[3].wait_recv()
+    multiply(held.at[1], yn)
+    copies[4].wait_recv()
+    copies[5].wait_recv()
+    multiply(held.at[2], dg)
+    for copy in copies:
+        copy.wait_send()
+
+
+def gather_project(tokens, in_weight):
+    rows, depth = tokens.shape
+    streams, _, width = in_weight.shape
+    tile = min(256, width)
+    parts = streams * (width // tile)
+    return pl.pallas_call(
+        project_kernel,
+        out_shape=jax.ShapeDtypeStruct((parts, 4 * rows, tile), jnp.bfloat16),
+        in_specs=[pl.BlockSpec(memory_space=pltpu.VMEM), pl.BlockSpec(memory_space=pl.ANY)],
+        out_specs=pl.BlockSpec(memory_space=pltpu.VMEM),
+        scratch_shapes=[
+            pltpu.VMEM((3, rows, depth), jnp.bfloat16),
+            pltpu.VMEM((parts, depth, tile), jnp.bfloat16),
+            pltpu.SemaphoreType.DMA((parts,)),
+            pltpu.SemaphoreType.DMA((6,)),
+            pltpu.SemaphoreType.DMA((6,)),
+        ],
+        compiler_params=pltpu.CompilerParams(
+            collective_id=0, has_side_effects=True, vmem_limit_bytes=VMEM_LIMIT
+        ),
+    )(tokens, in_weight)
+
+
+def tree_sum(values):
+    while len(values) > 1:
+        values = [a + b for a, b in zip(values[::2], values[1::2])] + (
+            [values[-1]] if len(values) % 2 else []
+        )
+    return values[0]
+
+
+def middle_kernel(
+    count, st_ref, taps_ref, rate_ref, res_ref, skip_ref, grad_ref, mixed_ref, gs_ref,
+    ext, side, prod, cgrad, conv, back, sgrad, halo, pole, carry_f, carry_b,
+    mine_f, mine_b, all_f, all_b, inc_f, inc_b,
+    send_f, recv_f, send_b, recv_b, send_h, recv_h,
+):
+    parts, length, tile = st_ref.shape
+    width = mixed_ref.shape[1]
+    per_stream = width // tile
+    modes = rate_ref.shape[0]
+    section = length // SUBLANES
+    chunks = length // ROWS
+    me = lax.axis_index("ctx")
+    after, prior = lax.rem(me + 1, count), lax.rem(me + count - 1, count)
+    greet("ctx", [lax.rem(me + step, count) for step in range(1, count)])
+
+    def neighbour(index, source, target, partner):
+        return pltpu.make_async_remote_copy(
+            src_ref=source,
+            dst_ref=target,
+            send_sem=send_h.at[index],
+            recv_sem=recv_h.at[index],
+            device_id={"ctx": partner},
+            device_id_type=MESH,
+        )
+
+    first = neighbour(0, st_ref.at[:, pl.ds(length - 16, 16), :], halo, after)
+    first.start()
+    pole[...] = jnp.exp(-rate_ref[...])
+
+    @pl.loop(0, chunks)
+    def _(step):
+        start = pl.multiple_of(step * ROWS, ROWS)
+        for part in range(parts):
+            ext[pl.ds(start + 8, ROWS), part * tile : (part + 1) * tile] = st_ref[
+                part, pl.ds(start, ROWS), :
+            ].astype(jnp.float32)
+
+    first.wait_recv()
+    keep = jnp.where(me > 0, 1.0, 0.0).astype(jnp.float32)
+    for part in range(parts):
+        ext[0:8, part * tile : (part + 1) * tile] = (
+            halo[part].astype(jnp.float32)[8:16] * keep
+        )
+
+    @pl.loop(0, chunks)
+    def _(step):
+        start = pl.multiple_of(step * ROWS, ROWS)
+        for col in range(0, width, LANES):
+            lanes = slice(col, col + LANES)
+            mixed = []
+            for s in range(3):
+                block = ext[pl.ds(start, ROWS + 8), s * width + col : s * width + col + LANES]
+                value = taps_ref[s, 0:1, lanes] * block[8:]
+                for j in range(1, 3):
+                    value = value + taps_ref[s, j : j + 1, lanes] * block[8 - j : 8 - j + ROWS]
+                side[s, pl.ds(start, ROWS), lanes] = value
+                mixed.append(value)
+            prod[col // LANES, pl.ds(start, ROWS), :] = mixed[1] * mixed[2]
+            cgrad[col // LANES, pl.ds(start, ROWS), :] = (
+                grad_ref[pl.ds(start, ROWS), lanes].astype(jnp.float32) * mixed[0]
+            )
+
+    tiles = width // LANES
+    sub = lax.broadcasted_iota(jnp.int32, (SUBLANES, LANES), 0)
+
+    def wide(ref, lanes):
+        return [
+            jnp.broadcast_to(ref[n : n + 1, lanes], (SUBLANES, LANES)) for n in range(modes)
+        ]
+
+    def local_scan(source, target, carry, mine, reverse):
+        @pl.loop(0, tiles)
+        def _(t):
+            lanes = pl.ds(pl.multiple_of(t * LANES, LANES), LANES)
+            p, r = wide(pole, lanes), wide(res_ref, lanes)
+
+            def body(i, state):
+                j = section - 1 - i if reverse else i
+                x = source[t, pl.ds(j, SUBLANES, stride=section), :]
+                state = [a * b + c * x for a, b, c in zip(p, state, r)]
+                target[t, pl.ds(j, SUBLANES, stride=section), :] = tree_sum(state)
+                return state
+
+            zero = jnp.zeros((SUBLANES, LANES), jnp.float32)
+            ends = lax.fori_loop(0, section, body, [zero] * modes, unroll=2)
+            for n in range(modes):
+                rate = rate_ref[n : n + 1, lanes]
+                total = ends[n]
+                for k in (1, 2, 4):
+                    decay = jnp.exp(rate * (-1.0 * section * k))
+                    moved = pltpu.roll(total, SUBLANES - k if reverse else k, 0)
+                    inside = sub < SUBLANES - k if reverse else sub >= k
+                    total = total + jnp.where(inside, decay * moved, 0.0)
+                moved = pltpu.roll(total, SUBLANES - 1 if reverse else 1, 0)
+                inside = sub < SUBLANES - 1 if reverse else sub >= 1
+                carry[n, :, lanes] = jnp.where(inside, moved, 0.0)
+                mine[n : n + 1, lanes] = total[0:1] if reverse else total[SUBLANES - 1 :]
+
+    def summary(mine, table, send_sem, recv_sem, source, partner):
+        return pltpu.make_async_remote_copy(
+            src_ref=mine,
+            dst_ref=table.at[source],
+            send_sem=send_sem.at[partner],
+            recv_sem=recv_sem.at[source],
+            device_id={"ctx": partner},
+            device_id_type=MESH,
+        )
+
+    forward = functools.partial(summary, mine_f, all_f, send_f, recv_f)
+    backward = functools.partial(summary, mine_b, all_b, send_b, recv_b)
+
+    local_scan(prod, conv, carry_f, mine_f, False)
+    for other in range(count):
+
+        @pl.when(other > me)
+        def _(other=other):
+            forward(me, other).start()
+
+    local_scan(cgrad, back, carry_b, mine_b, True)
+    for other in range(count):
+
+        @pl.when(other < me)
+        def _(other=other):
+            backward(me, other).start()
+
+    def add_carry(target, carry, incoming, reverse):
+        @pl.loop(0, tiles)
+        def _(t):
+            lanes = pl.ds(pl.multiple_of(t * LANES, LANES), LANES)
+            p = wide(pole, lanes)
+            steps = (SUBLANES - 1 - sub if reverse else sub).astype(jnp.float32) * (-1.0 * section)
+            state = [
+                carry[n, :, lanes]
+                + jnp.exp(rate_ref[n : n + 1, lanes] * steps) * incoming[n : n + 1, lanes]
+                for n in range(modes)
+            ]
+
+            def body(i, state):
+                j = section - 1 - i if reverse else i
+                state = [a * b for a, b in zip(p, state)]
+                place = pl.ds(j, SUBLANES, stride=section)
+                target[t, place, :] = target[t, place, :] + tree_sum(state)
+                return state
+
+            lax.fori_loop(0, section, body, state, unroll=2)
+
+    inc_f[...] = jnp.zeros_like(inc_f)
+    for other in range(count):
+
+        @pl.when(other < me)
+        def _(other=other):
+            forward(other, me).wait_recv()
+            gap = ((other + 1 - me) * length).astype(jnp.float32)
+            inc_f[...] += jnp.exp(rate_ref[...] * gap) * all_f[other]
+
+    add_carry(conv, carry_f, inc_f, False)
+    inc_b[...] = jnp.zeros_like(inc_b)
+    for other in range(count):
+
+        @pl.when(other > me)
+        def _(other=other):
+            backward(other, me).wait_recv()
+            gap = ((me + 1 - other) * length).astype(jnp.float32)
+            inc_b[...] += jnp.exp(rate_ref[...] * gap) * all_b[other]
+
+    add_carry(back, carry_b, inc_b, True)
+
+    def finish(start):
+        for col in range(0, width, LANES):
+            lanes = slice(col, col + LANES)
+            rows = pl.ds(start, ROWS)
+            skip = skip_ref[0:1, lanes]
+            filtered = conv[col // LANES, rows, :] + skip * prod[col // LANES, rows, :]
+            mixed_ref[rows, lanes] = (side[0, rows, lanes] * filtered).astype(mixed_ref.dtype)
+            product = back[col // LANES, rows, :] + skip * cgrad[col // LANES, rows, :]
+            upstream = grad_ref[rows, lanes].astype(jnp.float32)
+            sgrad[rows, lanes] = upstream * filtered
+            sgrad[rows, width + col : width + col + LANES] = product * side[2, rows, lanes]
+            sgrad[rows, 2 * width + col : 2 * width + col + LANES] = product * side[1, rows, lanes]
+
+    finish(0)
+    last = neighbour(1, sgrad.at[pl.ds(0, 8)], sgrad.at[pl.ds(length, 8)], prior)
+    last.start()
+
+    @pl.loop(1, chunks)
+    def _(step):
+        finish(pl.multiple_of(step * ROWS, ROWS))
+
+    def transpose_taps(start):
+        for s in range(3):
+            for col in range(0, width, LANES):
+                lanes = slice(s * width + col, s * width + col + LANES)
+                block = sgrad[pl.ds(start, ROWS + 8), lanes]
+                value = taps_ref[s, 0:1, col : col + LANES] * block[:ROWS]
+                for j in range(1, 3):
+                    value = value + taps_ref[s, j : j + 1, col : col + LANES] * block[j : j + ROWS]
+                gs_ref[pl.ds(start, ROWS), lanes] = value.astype(gs_ref.dtype)
+
+    @pl.loop(0, chunks - 1)
+    def _(step):
+        transpose_taps(pl.multiple_of(step * ROWS, ROWS))
+
+    last.wait_recv()
+
+    @pl.when(me == count - 1)
+    def _():
+        sgrad[length : length + 8, :] = jnp.zeros((8, 3 * width), jnp.float32)
+
+    transpose_taps(length - ROWS)
+    first.wait_send()
+    last.wait_send()
+    for other in range(count):
+
+        @pl.when(other > me)
+        def _(other=other):
+            forward(me, other).wait_send()
+
+        @pl.when(other < me)
+        def _(other=other):
+            backward(me, other).wait_send()
+
+
+def middle(streams, short_taps, decay_rate, residue, skip_gain, grad_out):
+    count = lax.axis_size("ctx")
+    parts, length, tile = streams.shape
+    modes, width = decay_rate.shape
+    f32 = jnp.float32
+    table = pltpu.VMEM((modes, width), f32)
+    tables = pltpu.VMEM((count, modes, width), f32)
+    plane = pltpu.VMEM((width // LANES, length, LANES), f32)
+    carry = pltpu.VMEM((modes, SUBLANES, width), f32)
+    dma = pltpu.SemaphoreType.DMA
+    return pl.pallas_call(
+        functools.partial(middle_kernel, count),
+        out_shape=(
+            jax.ShapeDtypeStruct((length, width), jnp.bfloat16),
+            jax.ShapeDtypeStruct((length, 3 * width), jnp.bfloat16),
+        ),
+        in_specs=vmem_specs(6),
+        out_specs=tuple(vmem_specs(2)),
+        scratch_shapes=[
+            pltpu.VMEM((length + 8, 3 * width), f32),
+            pltpu.VMEM((3, length, width), f32),
+            plane, plane, plane, plane,
+            pltpu.VMEM((length + 8, 3 * width), f32),
+            pltpu.VMEM((parts, 16, tile), jnp.bfloat16),
+            table, carry, carry, table, table, tables, tables, table, table,
+            dma((count,)), dma((count,)), dma((count,)), dma((count,)), dma((2,)), dma((2,)),
+        ],
+        compiler_params=pltpu.CompilerParams(
+            collective_id=1, has_side_effects=True, vmem_limit_bytes=VMEM_LIMIT
+        ),
+    )(streams, short_taps, decay_rate, residue, skip_gain[None], grad_out)
+
+
+def scatter_kernel(gs_ref, w_hbm, out_ref, w_buf, out_buf, in_buf, own, w_sem, send_sem, recv_sem):
+    rows, depth = out_ref.shape
+    pieces, streams, cols, width = w_buf.shape
+    half = pieces // 2
+    me, xn, yn, dg = square_partners()
+
+    def load(piece):
+        return pltpu.make_async_copy(
+            w_hbm.at[:, pl.ds(piece * cols, cols), :], w_buf.at[piece], w_sem.at[piece]
+        )
+
+    for piece in range(half):
+        load(piece).start()
+        load(half + piece).start()
+    greet("tp", (xn, yn))
+
+    def send(kind, piece, partner):
+        return pltpu.make_async_remote_copy(
+            src_ref=out_buf.at[kind, piece],
+            dst_ref=in_buf.at[kind, piece],
+            send_sem=send_sem.at[kind, piece],
+            recv_sem=recv_sem.at[kind, piece],
+            device_id={"tp": partner},
+            device_id_type=MESH,
+        )
+
+    def partial(owner, piece):
+        block = pl.ds(pl.multiple_of(owner * rows, rows), rows)
+        total = None
+        for s in range(streams):
+            term = lax.dot_general(
+                gs_ref[block, s * width : (s + 1) * width],
+                w_buf[piece, s],
+                (((1,), (1,)), ((), ())),
+                preferred_element_type=jnp.float32,
+            )
+            total = term if total is None else total + term
+        return total
+
+    def emit(kind, piece, value, partner):
+        out_buf[kind, piece] = value.astype(out_buf.dtype)
+        send(kind, piece, partner).start()
+
+    @pl.loop(0, half)
+    def _(k):
+        load(k).wait()
+        emit(0, k, partial(dg, k), xn)
+        load(half + k).wait()
+        emit(0, half + k, partial(dg, half + k), yn)
+
+    @pl.loop(0, half)
+    def _(k):
+        emit(1, k, partial(xn, k), xn)
+        emit(2, half + k, partial(yn, half + k), yn)
+
+    @pl.loop(0, half)
+    def _(k):
+        own_x, own_y = partial(xn, half + k), partial(yn, k)
+        send(0, half + k, yn).wait_recv()
+        emit(1, half + k, own_x + in_buf[0, half + k].astype(jnp.float32), xn)
+        send(0, k, xn).wait_recv()
+        emit(2, k, own_y + in_buf[0, k].astype(jnp.float32), yn)
+
+    @pl.loop(0, pieces)
+    def _(k):
+        own[k] = partial(me, k)
+
+    for k in [k + offset for k in range(half) for offset in (0, half)]:
+        send(1, k, xn).wait_recv()
+        send(2, k, yn).wait_recv()
+        out_ref[:, k * cols : (k + 1) * cols] = (
+            own[k] + in_buf[1, k].astype(jnp.float32) + in_buf[2, k].astype(jnp.float32)
+        ).astype(out_ref.dtype)
+    for k in range(pieces):
+        send(0, k, xn if k < half else yn).wait_send()
+        send(1, k, xn).wait_send()
+        send(2, k, yn).wait_send()
+
+
+def project_back(grad_streams, in_weight):
+    length = grad_streams.shape[0]
+    streams, depth, width = in_weight.shape
+    rows, pieces = length // 4, 8
+    cols = depth // pieces
+    travelling = pltpu.VMEM((3, pieces, rows, cols), jnp.bfloat16)
+    return pl.pallas_call(
+        scatter_kernel,
+        out_shape=jax.ShapeDtypeStruct((rows, depth), jnp.bfloat16),
+        in_specs=[pl.BlockSpec(memory_space=pltpu.VMEM), pl.BlockSpec(memory_space=pl.ANY)],
+        out_specs=pl.BlockSpec(memory_space=pltpu.VMEM),
+        scratch_shapes=[
+            pltpu.VMEM((pieces, streams, cols, width), jnp.bfloat16),
+            travelling,
+            travelling,
+            pltpu.VMEM((pieces, rows, cols), jnp.float32),
+            pltpu.SemaphoreType.DMA((pieces,)),
+            pltpu.SemaphoreType.DMA((3, pieces)),
+            pltpu.SemaphoreType.DMA((3, pieces)),
+        ],
+        compiler_params=pltpu.CompilerParams(
+            collective_id=2, has_side_effects=True, vmem_limit_bytes=VMEM_LIMIT
+        ),
+    )(grad_streams, in_weight)
+
+
+def square_shards(tokens, in_weight, short_taps, decay_rate, residue, skip_gain, grad_out):
+    streams = gather_project(tokens, in_weight)
+    mixed_out, grad_streams = middle(
+        streams, short_taps, decay_rate, residue, skip_gain, grad_out
+    )
+    return mixed_out, project_back(grad_streams, in_weight)
+
+
 def solution(mesh):
     in_specs = (
         P(("ctx", "tp"), None),
@@ -133,4 +627,5 @@
         P("ctx", "tp"),
     )
     out_specs = (P("ctx", "tp"), P(("ctx", "tp"), None))
-    return jax.shard_map(shards, mesh=mesh, in_specs=in_specs, out_specs=out_specs, check_vma=False)
+    body = square_shards if mesh.shape["tp"] == 4 else shards
+    return jax.shard_map(body, mesh=mesh, in_specs=in_specs, out_specs=out_specs, check_vma=False)

time: 433 us -> 118 us (0.27); the launches traced: 426 us -> 118 us
  matrix products: 131 us -> 0 us
  waiting for transfers between devices: 127 us -> 0 us
  Pallas kernels: 0 us -> 115 us
  local copies, waits for them, and re-layouts: 100 us -> 2.38 us
  blocking collectives: 28.9 us -> 0 us
  other arithmetic: 21.2 us -> 0 us
  between operations: 14.8 us -> 0.68 us
    dot_general x10 -> x0, matrix products: 131 us -> none  [the longest x2 60.7 us: modal_block(): jnp.einsum('abc,kbc->kac', toeplitz, sections, precision=exact_mode)]
    pallas_call x0 -> x3, Pallas kernels: none -> 115 us  [the longest x1 43.9 us: gather_project(): pl.pallas_call(project_kernel, out_shape=jax.ShapeDtypeStruct((parts, 4 *...]
    reduce_scatter x1 -> x0, waiting for transfers between devices: 86.9 us -> none  [shards(): lax.psum_scatter(jnp.einsum('rk,dk->rd', grad_streams, weight_cat, prefer...]
    all_gather x1 -> x0, waiting for transfers between devices: 38 us -> none  [shards(): lax.all_gather(tokens, 'tp', axis=0, tiled=True)]
    gather x2 -> x0, local copies, waits for them, and re-layouts: 33.1 us -> none  [modal_block(): filter_taps[jnp.maximum(lag_index, 0)]]
    all_gather x2 -> x0, blocking collectives: 28.9 us -> none  [the longest x1 14.7 us: shards(): lax.all_gather(backward_sum[None], 'ctx', axis=0, tiled=True)]
    rev x2 -> x0, local copies, waits for them, and re-layouts: 17.9 us -> none  [the longest x1 8.94 us: shards(): (backward_local + carry_term(incoming_bwd, log_pole, residue, length))[::-1]]
    squeeze x2 -> x0, local copies, waits for them, and re-layouts: 11.1 us -> none  [the longest x1 10.3 us: shards(): in_weight[0]]
  transfers between devices with their start and end apart: 4 -> 0, of which waited for: 3 -> 0; matrix products, arithmetic and copies ran while one was open for 12% -> 0% of each run, Pallas kernels for 0% -> 0%
where the time goes in v1:
time: 118 us
  Pallas kernels  115 us (97%)
  local copies, waits for them, and re-layouts  2.38 us (2%)
    pallas_call x1, Pallas kernels, gather_project(): pl.pallas_call(project_kernel, out_shape=jax.ShapeDtypeStruct((parts, 4 *...  43.9 us
    pallas_call x1, Pallas kernels, project_back(): pl.pallas_call(scatter_kernel, out_shape=jax.ShapeDtypeStruct((rows, dept...  41 us
    pallas_call x1, Pallas kernels, middle(): pl.pallas_call(functools.partial(middle_kernel, count), out_shape=(jax.Sh...  29.6 us
    unnamed x6, local copies, waits for them, and re-layouts  2.38 us

profile of v1, /device:TPU:0, one launch (start us, length us, event | category | flops | bytes accessed | tf_op | source)
XLA Modules:
  0.0 117.6 jit_solution(3076362248541488780)
XLA Ops:
  0.6 43.9 %shard_map.86.st_ref = bf16[6,512,256]{2,1,0:T(8,128)(2,1)} custom-call(bf16[128,4096]{1,0:T(8,128)(2,1)} %tok_ref.1, bf16[3,4096,512]{2,1,0:T(8,128)(2,1)} %w_hbm.3), custom_call_target="tpu_custom_call" | custom-call | tf_op jit(solution)/shard_map/pallas_call | solution.py:224
  44.5 29.6 %shard_map.87 = (bf16[512,512]{1,0:T(8,128)(2,1)}, bf16[512,1536]{1,0:T(8,128)(2,1)}) custom-call(bf16[6,512,256]{2,1,0:T(8,128)(2,1)} %shard_map.86.st_ref, f32[3,3,512]{2,1,0:T(4,128)} %taps_ref.1, f32[16,512]{1,0:T(8,128)} %rate_ref.1, f32[16,512]{1,0:T(8,128)} %res_ref.1, f32[1,512]{1,0:T(1,128)} %bitcast.1, bf16[512,512]{1,0:T(8,128)(2,1)} %grad_ref.1), custom_call_target="tpu_custom_call" | custom-call | tf_op jit(solution)/shard_map/pallas_call | solution.py:483
  74.2 0.0 copy-start.1
  74.2 41.0 %shard_map.88 = bf16[128,4096]{1,0:T(8,128)(2,1)} custom-call(bf16[512,1536]{1,0:T(8,128)(2,1)} %get-tuple-element.5.gs_ref, bf16[3,4096,512]{2,1,0:T(8,128)(2,1)} %w_hbm.3), custom_call_target="tpu_custom_call" | custom-call | tf_op jit(solution)/shard_map/pallas_call | solution.py:591
  115.2 0.0 copy-done.1
  115.2 0.0 copy-start
  115.2 0.8 copy.11
  116.0 0.6 copy-done
  116.6 1.0 copy.12
Async XLA Ops:
  74.2 41.0 %copy-start.1 = (bf16[512,512]{1,0:T(8,128)(2,1)S(1)}, bf16[512,512]{1,0:T(8,128)(2,1)}, u32[]{:S(2)}) copy-start(bf16[512,512]{1,0:T(8,128)(2,1)} %get-tuple-element.8) | copy-start | bytes 1572868
  115.2 1.4 %copy-start = (bf16[128,4096]{1,0:T(8,128)(2,1)S(1)}, bf16[128,4096]{1,0:T(8,128)(2,1)}, u32[]{:S(2)}) copy-start(bf16[128,4096]{1,0:T(8,128)(2,1)} %shard_map.88) | copy-start | bytes 3145732

commit v2 on v1

--- a/solution.py
+++ b/solution.py
@@ -143,16 +143,20 @@
     return me, y * 2 + (1 - x), (1 - y) * 2 + x, (1 - y) * 2 + (1 - x)
 
 
-def greet(axis, partners):
+def announce(axis, partners):
     barrier = pltpu.get_barrier_semaphore()
     for partner in partners:
         pl.semaphore_signal(barrier, inc=1, device_id={axis: partner}, device_id_type=MESH)
-    pl.semaphore_wait(barrier, len(partners))
+    return lambda: pl.semaphore_wait(barrier, len(partners))
+
+
+def greet(axis, partners):
+    announce(axis, partners)()
 
 
 def project_kernel(tok_ref, w_hbm, out_ref, held, w_buf, w_sem, send_sem, recv_sem):
     rows = tok_ref.shape[0]
-    half = rows // 2
+    half, part_rows = rows // 2, rows // 4
     width = w_hbm.shape[2]
     tile = w_buf.shape[2]
     per_stream = width // tile
@@ -170,7 +174,7 @@
     def send(index, source, slot, start, partner):
         return pltpu.make_async_remote_copy(
             src_ref=source,
-            dst_ref=held.at[slot, pl.ds(start, half)],
+            dst_ref=held.at[slot, pl.ds(start, source.shape[0])],
             send_sem=send_sem.at[index],
             recv_sem=recv_sem.at[index],
             device_id={"tp": partner},
@@ -183,8 +187,10 @@
         send(1, own_b, 1, half, yn),
         send(2, own_b, 0, half, xn),
         send(3, own_a, 1, 0, yn),
-        send(4, held.at[0, pl.ds(0, half)], 2, 0, yn),
-        send(5, held.at[1, pl.ds(half, half)], 2, half, xn),
+        send(4, held.at[0, pl.ds(0, part_rows)], 2, 0, yn),
+        send(5, held.at[1, pl.ds(half, part_rows)], 2, part_rows, xn),
+        send(6, held.at[0, pl.ds(part_rows, part_rows)], 2, half, yn),
+        send(7, held.at[1, pl.ds(half + part_rows, part_rows)], 2, half + part_rows, xn),
     ]
     for index in range(4):
         copies[index].start()
@@ -203,15 +209,29 @@
     multiply(tok_ref, me)
     copies[0].wait_recv()
     copies[4].start()
+    copies[6].start()
     copies[1].wait_recv()
     copies[5].start()
+    copies[7].start()
     copies[2].wait_recv()
     multiply(held.at[0], xn)
     copies[3].wait_recv()
     multiply(held.at[1], yn)
-    copies[4].wait_recv()
-    copies[5].wait_recv()
-    multiply(held.at[2], dg)
+    for step in range(2):
+        copies[4 + 2 * step].wait_recv()
+        copies[5 + 2 * step].wait_recv()
+        upper = pl.multiple_of(dg * rows + step * part_rows, part_rows)
+        lower = pl.multiple_of(dg * rows + half + step * part_rows, part_rows)
+        block = held.at[2, pl.ds(step * half, half)]
+
+        @pl.loop(0, 3 * per_stream)
+        def _(part, block=block, upper=upper, lower=lower):
+            value = jnp.dot(
+                block[...], w_buf[part], preferred_element_type=jnp.float32
+            ).astype(out_ref.dtype)
+            out_ref[part, pl.ds(upper, part_rows), :] = value[:part_rows]
+            out_ref[part, pl.ds(lower, part_rows), :] = value[part_rows:]
+
     for copy in copies:
         copy.wait_send()
 
@@ -230,8 +250,8 @@
             pltpu.VMEM((3, rows, depth), jnp.bfloat16),
             pltpu.VMEM((parts, depth, tile), jnp.bfloat16),
             pltpu.SemaphoreType.DMA((parts,)),
-            pltpu.SemaphoreType.DMA((6,)),
-            pltpu.SemaphoreType.DMA((6,)),
+            pltpu.SemaphoreType.DMA((8,)),
+            pltpu.SemaphoreType.DMA((8,)),
         ],
         compiler_params=pltpu.CompilerParams(
             collective_id=0, has_side_effects=True, vmem_limit_bytes=VMEM_LIMIT
@@ -261,7 +281,7 @@
     chunks = length // ROWS
     me = lax.axis_index("ctx")
     after, prior = lax.rem(me + 1, count), lax.rem(me + count - 1, count)
-    greet("ctx", [lax.rem(me + step, count) for step in range(1, count)])
+    entered = announce("ctx", [lax.rem(me + step, count) for step in range(1, count)])
 
     def neighbour(index, source, target, partner):
         return pltpu.make_async_remote_copy(
@@ -274,7 +294,6 @@
         )
 
     first = neighbour(0, st_ref.at[:, pl.ds(length - 16, 16), :], halo, after)
-    first.start()
     pole[...] = jnp.exp(-rate_ref[...])
 
     @pl.loop(0, chunks)
@@ -285,16 +304,10 @@
                 part, pl.ds(start, ROWS), :
             ].astype(jnp.float32)
 
-    first.wait_recv()
-    keep = jnp.where(me > 0, 1.0, 0.0).astype(jnp.float32)
-    for part in range(parts):
-        ext[0:8, part * tile : (part + 1) * tile] = (
-            halo[part].astype(jnp.float32)[8:16] * keep
-        )
-
-    @pl.loop(0, chunks)
-    def _(step):
-        start = pl.multiple_of(step * ROWS, ROWS)
+    entered()
+    first.start()
+
+    def short_mix(start):
         for col in range(0, width, LANES):
             lanes = slice(col, col + LANES)
             mixed = []
@@ -310,6 +323,19 @@
                 grad_ref[pl.ds(start, ROWS), lanes].astype(jnp.float32) * mixed[0]
             )
 
+    @pl.loop(1, chunks)
+    def _(step):
+        short_mix(pl.multiple_of(step * ROWS, ROWS))
+
+    first.wait_recv()
+    keep = jnp.where(me > 0, 1.0, 0.0).astype(jnp.float32)
+    for part in range(parts):
+        ext[0:8, part * tile : (part + 1) * tile] = (
+            halo[part].astype(jnp.float32)[8:16] * keep
+        )
+
+    short_mix(0)
+
     tiles = width // LANES
     sub = lax.broadcasted_iota(jnp.int32, (SUBLANES, LANES), 0)
 
@@ -318,24 +344,22 @@
             jnp.broadcast_to(ref[n : n + 1, lanes], (SUBLANES, LANES)) for n in range(modes)
         ]
 
-    def local_scan(source, target, carry, mine, reverse):
+    def end_states(source, carry, mine, reverse):
         @pl.loop(0, tiles)
         def _(t):
             lanes = pl.ds(pl.multiple_of(t * LANES, LANES), LANES)
-            p, r = wide(pole, lanes), wide(res_ref, lanes)
+            p = wide(pole, lanes)
 
             def body(i, state):
                 j = section - 1 - i if reverse else i
                 x = source[t, pl.ds(j, SUBLANES, stride=section), :]
-                state = [a * b + c * x for a, b, c in zip(p, state, r)]
-                target[t, pl.ds(j, SUBLANES, stride=section), :] = tree_sum(state)
-                return state
+                return [a * b + x for a, b in zip(p, state)]
 
             zero = jnp.zeros((SUBLANES, LANES), jnp.float32)
-            ends = lax.fori_loop(0, section, body, [zero] * modes, unroll=2)
+            ends = lax.fori_loop(0, section, body, [zero] * modes, unroll=4)
             for n in range(modes):
                 rate = rate_ref[n : n + 1, lanes]
-                total = ends[n]
+                total = ends[n] * res_ref[n : n + 1, lanes]
                 for k in (1, 2, 4):
                     decay = jnp.exp(rate * (-1.0 * section * k))
                     moved = pltpu.roll(total, SUBLANES - k if reverse else k, 0)
@@ -346,6 +370,22 @@
                 carry[n, :, lanes] = jnp.where(inside, moved, 0.0)
                 mine[n : n + 1, lanes] = total[0:1] if reverse else total[SUBLANES - 1 :]
 
+    def local_scan(source, target, carry, reverse):
+        @pl.loop(0, tiles)
+        def _(t):
+            lanes = pl.ds(pl.multiple_of(t * LANES, LANES), LANES)
+            p, r = wide(pole, lanes), wide(res_ref, lanes)
+
+            def body(i, state):
+                j = section - 1 - i if reverse else i
+                x = source[t, pl.ds(j, SUBLANES, stride=section), :]
+                state = [a * b + c * x for a, b, c in zip(p, state, r)]
+                target[t, pl.ds(j, SUBLANES, stride=section), :] = tree_sum(state)
+                return state
+
+            start = [carry[n, :, lanes] for n in range(modes)]
+            lax.fori_loop(0, section, body, start, unroll=2)
+
     def summary(mine, table, send_sem, recv_sem, source, partner):
         return pltpu.make_async_remote_copy(
             src_ref=mine,
@@ -359,29 +399,31 @@
     forward = functools.partial(summary, mine_f, all_f, send_f, recv_f)
     backward = functools.partial(summary, mine_b, all_b, send_b, recv_b)
 
-    local_scan(prod, conv, carry_f, mine_f, False)
+    end_states(prod, carry_f, mine_f, False)
     for other in range(count):
 
         @pl.when(other > me)
         def _(other=other):
             forward(me, other).start()
 
-    local_scan(cgrad, back, carry_b, mine_b, True)
+    end_states(cgrad, carry_b, mine_b, True)
     for other in range(count):
 
         @pl.when(other < me)
         def _(other=other):
             backward(me, other).start()
 
-    def add_carry(target, carry, incoming, reverse):
+    local_scan(prod, conv, carry_f, False)
+    local_scan(cgrad, back, carry_b, True)
+
+    def add_carry(target, incoming, reverse):
         @pl.loop(0, tiles)
         def _(t):
             lanes = pl.ds(pl.multiple_of(t * LANES, LANES), LANES)
             p = wide(pole, lanes)
             steps = (SUBLANES - 1 - sub if reverse else sub).astype(jnp.float32) * (-1.0 * section)
             state = [
-                carry[n, :, lanes]
-                + jnp.exp(rate_ref[n : n + 1, lanes] * steps) * incoming[n : n + 1, lanes]
+                jnp.exp(rate_ref[n : n + 1, lanes] * steps) * incoming[n : n + 1, lanes]
                 for n in range(modes)
             ]
 
@@ -403,7 +445,7 @@
             gap = ((other + 1 - me) * length).astype(jnp.float32)
             inc_f[...] += jnp.exp(rate_ref[...] * gap) * all_f[other]
 
-    add_carry(conv, carry_f, inc_f, False)
+    add_carry(conv, inc_f, False)
     inc_b[...] = jnp.zeros_like(inc_b)
     for other in range(count):
 
@@ -413,7 +455,7 @@
             gap = ((me + 1 - other) * length).astype(jnp.float32)
             inc_b[...] += jnp.exp(rate_ref[...] * gap) * all_b[other]
 
-    add_carry(back, carry_b, inc_b, True)
+    add_carry(back, inc_b, True)
 
     def finish(start):
         for col in range(0, width, LANES):
@@ -517,7 +559,7 @@
     for piece in range(half):
         load(piece).start()
         load(half + piece).start()
-    greet("tp", (xn, yn))
+    entered = announce("tp", (xn, yn))
 
     def send(kind, piece, partner):
         return pltpu.make_async_remote_copy(
@@ -546,7 +588,14 @@
         out_buf[kind, piece] = value.astype(out_buf.dtype)
         send(kind, piece, partner).start()
 
-    @pl.loop(0, half)
+    load(0).wait()
+    opening = partial(dg, 0)
+    entered()
+    emit(0, 0, opening, xn)
+    load(half).wait()
+    emit(0, half, partial(dg, half), yn)
+
+    @pl.loop(1, half)
     def _(k):
         load(k).wait()
         emit(0, k, partial(dg, k), xn)

time: 118 us -> 118 us (level)
  no operation moved by 1% of the time
where the time goes in v2:
time: 118 us; the launch traced here: 117 us
  Pallas kernels  114 us (97%)
  local copies, waits for them, and re-layouts  2.38 us (2%)
    pallas_call x1, Pallas kernels, gather_project(): pl.pallas_call(project_kernel, out_shape=jax.ShapeDtypeStruct((parts, 4 *...  44.1 us
    pallas_call x1, Pallas kernels, project_back(): pl.pallas_call(scatter_kernel, out_shape=jax.ShapeDtypeStruct((rows, dept...  40.5 us
    pallas_call x1, Pallas kernels, middle(): pl.pallas_call(functools.partial(middle_kernel, count), out_shape=(jax.Sh...  29.4 us
    unnamed x6, local copies, waits for them, and re-layouts  2.38 us

profile of v2, /device:TPU:0, one launch (start us, length us, event | category | flops | bytes accessed | tf_op | source)
XLA Modules:
  0.0 117.0 jit_solution(15371468929123186002)
XLA Ops:
  0.6 44.1 %shard_map.86.st_ref = bf16[6,512,256]{2,1,0:T(8,128)(2,1)} custom-call(bf16[128,4096]{1,0:T(8,128)(2,1)} %tok_ref.1, bf16[3,4096,512]{2,1,0:T(8,128)(2,1)} %w_hbm.3), custom_call_target="tpu_custom_call" | custom-call | tf_op jit(solution)/shard_map/pallas_call | solution.py:244
  44.8 29.4 %shard_map.87 = (bf16[512,512]{1,0:T(8,128)(2,1)}, bf16[512,1536]{1,0:T(8,128)(2,1)}) custom-call(bf16[6,512,256]{2,1,0:T(8,128)(2,1)} %shard_map.86.st_ref, f32[3,3,512]{2,1,0:T(4,128)} %taps_ref.1, f32[16,512]{1,0:T(8,128)} %rate_ref.1, f32[16,512]{1,0:T(8,128)} %res_ref.1, f32[1,512]{1,0:T(1,128)} %bitcast.1, bf16[512,512]{1,0:T(8,128)(2,1)} %grad_ref.1), custom_call_target="tpu_custom_call" | custom-call | tf_op jit(solution)/shard_map/pallas_call | solution.py:525
  74.2 0.0 copy-start.1
  74.2 40.5 %shard_map.88 = bf16[128,4096]{1,0:T(8,128)(2,1)} custom-call(bf16[512,1536]{1,0:T(8,128)(2,1)} %get-tuple-element.5.gs_ref, bf16[3,4096,512]{2,1,0:T(8,128)(2,1)} %w_hbm.3), custom_call_target="tpu_custom_call" | custom-call | tf_op jit(solution)/shard_map/pallas_call | solution.py:640
  114.6 0.0 copy-done.1
  114.6 0.0 copy-start
  114.7 0.8 copy.11
  115.5 0.6 copy-done
  116.1 1.0 copy.12
Async XLA Ops:
  74.2 40.5 %copy-start.1 = (bf16[512,512]{1,0:T(8,128)(2,1)S(1)}, bf16[512,512]{1,0:T(8,128)(2,1)}, u32[]{:S(2)}) copy-start(bf16[512,512]{1,0:T(8,128)(2,1)} %get-tuple-element.8) | copy-start | bytes 1572868
  114.6 1.4 %copy-start = (bf16[128,4096]{1,0:T(8,128)(2,1)S(1)}, bf16[128,4096]{1,0:T(8,128)(2,1)}, u32[]{:S(2)}) copy-start(bf16[128,4096]{1,0:T(8,128)(2,1)} %shard_map.88) | copy-start | bytes 3145732

commit v3 on v2

--- a/solution.py
+++ b/solution.py
@@ -370,7 +370,14 @@
                 carry[n, :, lanes] = jnp.where(inside, moved, 0.0)
                 mine[n : n + 1, lanes] = total[0:1] if reverse else total[SUBLANES - 1 :]
 
-    def local_scan(source, target, carry, reverse):
+    def incoming_at(incoming, lanes, reverse):
+        steps = (SUBLANES - 1 - sub if reverse else sub).astype(jnp.float32) * (-1.0 * section)
+        return [
+            jnp.exp(rate_ref[n : n + 1, lanes] * steps) * incoming[n : n + 1, lanes]
+            for n in range(modes)
+        ]
+
+    def local_scan(source, target, carry, incoming, reverse):
         @pl.loop(0, tiles)
         def _(t):
             lanes = pl.ds(pl.multiple_of(t * LANES, LANES), LANES)
@@ -384,6 +391,9 @@
                 return state
 
             start = [carry[n, :, lanes] for n in range(modes)]
+            if incoming is not None:
+                arrived = incoming_at(incoming, lanes, reverse)
+                start = [a + b for a, b in zip(start, arrived)]
             lax.fori_loop(0, section, body, start, unroll=2)
 
     def summary(mine, table, send_sem, recv_sem, source, partner):
@@ -399,6 +409,13 @@
     forward = functools.partial(summary, mine_f, all_f, send_f, recv_f)
     backward = functools.partial(summary, mine_b, all_b, send_b, recv_b)
 
+    end_states(cgrad, carry_b, mine_b, True)
+    for other in range(count):
+
+        @pl.when(other < me)
+        def _(other=other):
+            backward(me, other).start()
+
     end_states(prod, carry_f, mine_f, False)
     for other in range(count):
 
@@ -406,26 +423,14 @@
         def _(other=other):
             forward(me, other).start()
 
-    end_states(cgrad, carry_b, mine_b, True)
-    for other in range(count):
-
-        @pl.when(other < me)
-        def _(other=other):
-            backward(me, other).start()
-
-    local_scan(prod, conv, carry_f, False)
-    local_scan(cgrad, back, carry_b, True)
+    local_scan(prod, conv, carry_f, None, False)
 
     def add_carry(target, incoming, reverse):
         @pl.loop(0, tiles)
         def _(t):
             lanes = pl.ds(pl.multiple_of(t * LANES, LANES), LANES)
             p = wide(pole, lanes)
-            steps = (SUBLANES - 1 - sub if reverse else sub).astype(jnp.float32) * (-1.0 * section)
-            state = [
-                jnp.exp(rate_ref[n : n + 1, lanes] * steps) * incoming[n : n + 1, lanes]
-                for n in range(modes)
-            ]
+            state = incoming_at(incoming, lanes, reverse)
 
             def body(i, state):
                 j = section - 1 - i if reverse else i
@@ -436,6 +441,16 @@
 
             lax.fori_loop(0, section, body, state, unroll=2)
 
+    inc_b[...] = jnp.zeros_like(inc_b)
+    for other in range(count):
+
+        @pl.when(other > me)
+        def _(other=other):
+            backward(other, me).wait_recv()
+            gap = ((me + 1 - other) * length).astype(jnp.float32)
+            inc_b[...] += jnp.exp(rate_ref[...] * gap) * all_b[other]
+
+    local_scan(cgrad, back, carry_b, inc_b, True)
     inc_f[...] = jnp.zeros_like(inc_f)
     for other in range(count):
 
@@ -446,16 +461,7 @@
             inc_f[...] += jnp.exp(rate_ref[...] * gap) * all_f[other]
 
     add_carry(conv, inc_f, False)
-    inc_b[...] = jnp.zeros_like(inc_b)
-    for other in range(count):
-
-        @pl.when(other > me)
-        def _(other=other):
-            backward(other, me).wait_recv()
-            gap = ((me + 1 - other) * length).astype(jnp.float32)
-            inc_b[...] += jnp.exp(rate_ref[...] * gap) * all_b[other]
-
-    add_carry(back, inc_b, True)
+
 
     def finish(start):
         for col in range(0, width, LANES):

time: 118 us -> 114 us (0.966)
  Pallas kernels: 114 us -> 110 us
    pallas_call x1, Pallas kernels: 29.4 us -> 25.8 us  [middle(): pl.pallas_call(functools.partial(middle_kernel, count), out_shape=(jax.Sh...]
where the time goes in v3:
time: 114 us; the launch traced here: 113 us
  Pallas kernels  110 us (96%)
  local copies, waits for them, and re-layouts  2.38 us (2%)
    pallas_call x1, Pallas kernels, gather_project(): pl.pallas_call(project_kernel, out_shape=jax.ShapeDtypeStruct((parts, 4 *...  44.1 us
    pallas_call x1, Pallas kernels, project_back(): pl.pallas_call(scatter_kernel, out_shape=jax.ShapeDtypeStruct((rows, dept...  40.4 us
    pallas_call x1, Pallas kernels, middle(): pl.pallas_call(functools.partial(middle_kernel, count), out_shape=(jax.Sh...  25.8 us
    unnamed x6, local copies, waits for them, and re-layouts  2.38 us

profile of v3, /device:TPU:0, one launch (start us, length us, event | category | flops | bytes accessed | tf_op | source)
XLA Modules:
  0.0 113.5 jit_solution(10686981716389543108)
XLA Ops:
  0.6 44.1 %shard_map.86.st_ref = bf16[6,512,256]{2,1,0:T(8,128)(2,1)} custom-call(bf16[128,4096]{1,0:T(8,128)(2,1)} %tok_ref.1, bf16[3,4096,512]{2,1,0:T(8,128)(2,1)} %w_hbm.3), custom_call_target="tpu_custom_call" | custom-call | tf_op jit(solution)/shard_map/pallas_call | solution.py:244
  44.8 25.8 %shard_map.87 = (bf16[512,512]{1,0:T(8,128)(2,1)}, bf16[512,1536]{1,0:T(8,128)(2,1)}) custom-call(bf16[6,512,256]{2,1,0:T(8,128)(2,1)} %shard_map.86.st_ref, f32[3,3,512]{2,1,0:T(4,128)} %taps_ref.1, f32[16,512]{1,0:T(8,128)} %rate_ref.1, f32[16,512]{1,0:T(8,128)} %res_ref.1, f32[1,512]{1,0:T(1,128)} %bitcast.1, bf16[512,512]{1,0:T(8,128)(2,1)} %grad_ref.1), custom_call_target="tpu_custom_call" | custom-call | tf_op jit(solution)/shard_map/pallas_call | solution.py:531
  70.6 0.0 copy-start.1
  70.6 40.4 %shard_map.88 = bf16[128,4096]{1,0:T(8,128)(2,1)} custom-call(bf16[512,1536]{1,0:T(8,128)(2,1)} %get-tuple-element.5.gs_ref, bf16[3,4096,512]{2,1,0:T(8,128)(2,1)} %w_hbm.3), custom_call_target="tpu_custom_call" | custom-call | tf_op jit(solution)/shard_map/pallas_call | solution.py:646
  111.1 0.0 copy-done.1
  111.1 0.0 copy-start
  111.1 0.8 copy.11
  111.9 0.6 copy-done
  112.5 1.0 copy.12
Async XLA Ops:
  70.6 40.5 %copy-start.1 = (bf16[512,512]{1,0:T(8,128)(2,1)S(1)}, bf16[512,512]{1,0:T(8,128)(2,1)}, u32[]{:S(2)}) copy-start(bf16[512,512]{1,0:T(8,128)(2,1)} %get-tuple-element.8) | copy-start | bytes 1572868
  111.1 1.4 %copy-start = (bf16[128,4096]{1,0:T(8,128)(2,1)S(1)}, bf16[128,4096]{1,0:T(8,128)(2,1)}, u32[]{:S(2)}) copy-start(bf16[128,4096]{1,0:T(8,128)(2,1)} %shard_map.88) | copy-start | bytes 3145732
